TPU v7x, 256 devices: a whole 4x4x8 slice. The times are simulated.
256 devices in a mesh: cfg: 8 (over y, core), node: 32 (over z, x).
Axes of the slice: x: 4, y: 4, z: 8, core: 2. Of those that a mesh axis runs over, the one named last changes fastest.
Arguments:
- node_feats: bfloat16 [1048576, 256], P(('cfg', 'node')), may hold values from -6 to 6
- neighbors: int32 [1048576, 4], P(('cfg', 'node')), may hold values from 0 to 5119
- self_weight: bfloat16 [256, 256], replicated, may hold values from -0.375 to 0.375
- neighbor_weight: bfloat16 [256, 256], replicated, may hold values from -0.375 to 0.375
- sage_bias: float32 [256], replicated, may hold values from -3 to 3
- conf_index: int32 [32768], P(('cfg', 'node')), may hold values from 0 to 4095
- layout_ids: int32 [128, 32768], P('cfg', 'node'), may hold values from 0 to 127
- join_weight: bfloat16 [256, 256], replicated, may hold values from -0.375 to 0.375
- layout_table: bfloat16 [128, 256], replicated, may hold values from -6 to 6
- join_bias: float32 [256], replicated, may hold values from -3 to 3
- mid_weight: bfloat16 [256, 256], replicated, may hold values from -0.375 to 0.375
- mid_bias: float32 [256], replicated, may hold values from -3 to 3
- score_weight: float32 [256], replicated, may hold values from -0.375 to 0.375
- config_pairs: int32 [512, 2], replicated, may hold values from 0 to 127
Outputs:
- node_embed: bfloat16 [1048576, 256], P(('cfg', 'node'))
- pair_loss: float32 [], replicated
- conf_grad: float32 [32768, 256], P(('cfg', 'node'))
All inputs are finite; a program needn't handle non-finite values.
Results may differ from a plain program's by a relative error of at most 0.028.
Values may be sent and summed in bfloat16 or wider, within the bound.
No kernel may reach another device: no remote copies, remote signals or barrier semaphores. Data moves between devices by JAX's collectives and lax.ppermute only.
A program may use at most 64 MiB of HBM per device.

v0:
```python
import math
import jax
import jax.numpy as jnp
from jax import lax
from jax.sharding import PartitionSpec as P

HALO = 512


def with_halo(value, sides, width):
    for axis, dim in sides:
        size, length = (lax.axis_size(axis), value.shape[dim])
        up = [(i, (i + 1) % size) for i in range(size - 1)]
        down = [(j, i) for i, j in up]
        last = lax.slice_in_dim(value, length - width, length, axis=dim)
        leading = lax.slice_in_dim(value, 0, width, axis=dim)
        before = lax.ppermute(last, axis, up)
        after = lax.ppermute(leading, axis, down)
        value = jnp.concatenate([before, value, after], axis=dim)
    return value


def silu_slope(value):
    sigma = jax.nn.sigmoid(value)
    return sigma * (1.0 + value * (1.0 - sigma))


def pair_terms(config_score, config_pairs):
    config_total_count = config_score.shape[0]
    pair_first = config_pairs[:, 0]
    pair_second = config_pairs[:, 1]
    score_gap = jnp.take(config_score, pair_second) - jnp.take(config_score, pair_first)
    pair_loss = jnp.mean(jax.nn.softplus(score_gap))
    pair_slope = jax.nn.sigmoid(score_gap) / config_pairs.shape[0]
    columns = jnp.arange(config_total_count, dtype=jnp.int32)
    signed = (pair_second[:, None] == columns[None, :]).astype(jnp.float32) - (
        pair_first[:, None] == columns[None, :]
    ).astype(jnp.float32)
    score_grad = 65536.0 * jnp.dot(pair_slope, signed, precision=lax.Precision.HIGHEST)
    return (pair_loss, score_grad)


def shards(
    node_feats,
    neighbors,
    self_weight,
    neighbor_weight,
    sage_bias,
    conf_index,
    layout_ids,
    join_weight,
    layout_table,
    join_bias,
    mid_weight,
    mid_bias,
    score_weight,
    config_pairs,
):
    node_rows = node_feats.shape[0]
    feat_width = node_feats.shape[1]
    hidden_width = join_weight.shape[1]
    padded = with_halo(node_feats, ((("cfg", "node"), 0),), HALO)
    summed = jnp.zeros((node_rows, feat_width), jnp.float32)
    for neighbor in range(neighbors.shape[1]):
        summed = summed + jnp.take(padded, neighbors[:, neighbor], axis=0).astype(jnp.float32)
    neighbour_mean = (summed / neighbors.shape[1]).astype(jnp.bfloat16)
    pre_act = (
        jnp.dot(node_feats, self_weight, preferred_element_type=jnp.float32)
        + jnp.dot(neighbour_mean, neighbor_weight, preferred_element_type=jnp.float32)
        + sage_bias
    )
    node_embed = jax.nn.silu(pre_act).astype(jnp.bfloat16)
    conf_src = jnp.take(node_embed, conf_index, axis=0)
    node_count = lax.axis_size("node")
    group_count = lax.axis_size("cfg")
    local_conf = conf_index.shape[0]
    per_peer = local_conf // node_count
    local_configs = layout_ids.shape[0]
    norm_scale = 1.0 / math.sqrt(layout_ids.shape[1] * node_count)
    table_ids = jnp.arange(layout_table.shape[0], dtype=jnp.int32)

    def hidden_rows(base_rows, row_ids):
        picks = (row_ids[:, None] == table_ids[None, :]).astype(jnp.bfloat16)
        inner_pre = (
            base_rows + jnp.dot(picks, layout_table, preferred_element_type=jnp.float32) + join_bias
        )
        inner_act = jax.nn.silu(inner_pre).astype(jnp.bfloat16)
        outer_pre = jnp.dot(inner_act, mid_weight, preferred_element_type=jnp.float32) + mid_bias
        return (inner_pre, outer_pre)

    grouped = lax.all_gather(conf_src, "cfg", axis=0, tiled=True)
    spread = lax.all_to_all(
        grouped.reshape(group_count, node_count, per_peer, feat_width),
        "node",
        split_axis=1,
        concat_axis=1,
        tiled=True,
    )
    conf_rows = spread.reshape(-1, feat_width)
    row_count = conf_rows.shape[0]
    base = jnp.dot(conf_rows, join_weight, preferred_element_type=jnp.float32)

    def config_total(row_ids):
        inner_pre, outer_pre = hidden_rows(base, row_ids)
        scores = jnp.dot(jax.nn.silu(outer_pre), score_weight, precision=lax.Precision.HIGHEST)
        return jnp.sum(scores)

    partial_sums = lax.map(config_total, layout_ids)
    local_score = lax.psum(partial_sums, "node") * norm_scale
    config_score = lax.all_gather(local_score, "cfg", axis=0, tiled=True)
    pair_loss, score_grad = pair_terms(config_score, config_pairs)
    local_grads = lax.dynamic_slice_in_dim(
        score_grad, lax.axis_index("cfg") * local_configs, local_configs, 0
    )

    def config_step(carried, inputs):
        row_ids, config_grad = inputs
        inner_pre, outer_pre = hidden_rows(base, row_ids)
        outer_grad = (config_grad * norm_scale * score_weight * silu_slope(outer_pre)).astype(
            jnp.bfloat16
        )
        inner_grad = lax.dot_general(
            outer_grad, mid_weight, (((1,), (1,)), ((), ())), preferred_element_type=jnp.float32
        ) * silu_slope(inner_pre)
        return (carried + inner_grad, None)

    zero_rows = jnp.zeros((row_count, hidden_width), jnp.float32)
    group_part, unused = lax.scan(config_step, zero_rows, (layout_ids, local_grads))
    row_sum = lax.psum_scatter(
        group_part.astype(jnp.bfloat16), "cfg", scatter_dimension=0, tiled=True
    )
    local_grad = lax.dot_general(
        row_sum, join_weight, (((1,), (1,)), ((), ())), preferred_element_type=jnp.float32
    )
    returned = lax.all_to_all(
        local_grad.reshape(node_count, per_peer, feat_width).astype(jnp.bfloat16),
        "node",
        split_axis=0,
        concat_axis=0,
        tiled=True,
    ).astype(jnp.float32)
    conf_grad = returned.reshape(-1, feat_width)
    return (node_embed, pair_loss, conf_grad)


def solution(mesh):
    placed = (
        P(("cfg", "node"), None),
        P(("cfg", "node"), None),
        P(),
        P(),
        P(),
        P(("cfg", "node")),
        P("cfg", "node"),
        P(),
        P(),
        P(),
        P(),
        P(),
        P(),
        P(),
    )
    return jax.shard_map(
        shards,
        mesh=mesh,
        in_specs=placed,
        out_specs=(P(("cfg", "node"), None), P(), P(("cfg", "node"), None)),
        check_vma=False,
    )
```

profile of v0, /device:TPU:2, one launch (start us, length us, event | category | flops | bytes accessed | tf_op | source)
XLA Modules:
  0.0 480.4 jit_solution(4784900319033597347)
XLA Ops:
  8.3 3.4 collective-permute-start
  16.6 4.4 fusion.62
  21.4 17.0 %gather_fusion.4 = bf16[4096,256]{1,0:T(8,128)(2,1)} fusion(bf16[5120,256]{1,0:T(8,128)(2,1)S(1)} %constant_dynamic-update-slice_fusion, s32[4096]{0:T(1024)S(1)} %fusion.55), kind=kCustom, calls=%fused_computation.4.clone | custom fusion | bytes 4210688 | tf_op jit(solution)/shard_map/jit(_take)/gather | solution.py:65
  38.4 16.9 %gather_fusion.1 = bf16[4096,256]{1,0:T(8,128)(2,1)} fusion(bf16[5120,256]{1,0:T(8,128)(2,1)S(1)} %constant_dynamic-update-slice_fusion, s32[4096]{0:T(1024)S(1)} %fusion.52), kind=kCustom, calls=%fused_computation.clone | custom fusion | bytes 4210688 | tf_op jit(solution)/shard_map/jit(_take)/gather | solution.py:65
  55.3 16.9 %gather_fusion.2 = bf16[4096,256]{1,0:T(8,128)(2,1)} fusion(bf16[5120,256]{1,0:T(8,128)(2,1)S(1)} %constant_dynamic-update-slice_fusion, s32[4096]{0:T(1024)S(1)} %fusion.53), kind=kCustom, calls=%fused_computation.2.clone | custom fusion | bytes 4210688 | tf_op jit(solution)/shard_map/jit(_take)/gather | solution.py:65
  72.2 16.9 %gather_fusion.3 = bf16[4096,256]{1,0:T(8,128)(2,1)} fusion(bf16[5120,256]{1,0:T(8,128)(2,1)S(1)} %constant_dynamic-update-slice_fusion, s32[4096]{0:T(1024)S(1)} %fusion.54), kind=kCustom, calls=%fused_computation.3.clone | custom fusion | bytes 4210688 | tf_op jit(solution)/shard_map/jit(_take)/gather | solution.py:65
  89.1 8.0 %multiply_convert_fusion.5 = bf16[4096,256]{1,0:T(8,128)(2,1)S(1)} fusion(f32[4096,256]{1,0:T(8,128)} %fusion.62, bf16[256,256]{1,0:T(8,128)(2,1)S(1)} %copy-done.8, bf16[4096,256]{1,0:T(8,128)(2,1)} %gather_fusion.4, bf16[4096,256]{1,0:T(8,128)(2,1)} %gather_fusion.3, bf16[4096,256]{1,0:T(8,128)(2,1)} %gather_fusion.2, ...), kind=kOutput, calls=%fused_computation.48 | convolution fusion | flops 557842432 | bytes 14828544 | tf_op jit(solution)/shard_map/dot_general | solution.py:69
  98.6 13.6 %all_gather.6 = bf16[1024,256]{1,0:T(8,128)(2,1)S(1)} all-gather(bf16[128,256]{1,0:T(8,128)(2,1)S(1)} %broadcast_select_fusion), channel_id=1, replica_groups=mesh['cfg'=8,'node'=32] {'cfg'}, dimensions={0}, use_global_device_ids=true | all-gather | bytes 589824 | tf_op jit(solution)/shard_map/all_gather | solution.py:91
  113.4 13.7 %all-to-all-start = ((bf16[8,32,4,256]{3,2,0,1:T(4,128)(2,1)}), bf16[8,32,4,256]{3,2,0,1:T(4,128)(2,1)S(1)}, u32[]{:S(2)}, u32[]{:S(2)}) async-start(bf16[8,32,4,256]{3,2,0,1:T(4,128)(2,1)} %copy.18), calls=%async_computation | async-start | bytes 1048576 | tf_op jit(solution)/shard_map/all_to_all | solution.py:92
  128.5 15.9 %all-to-all-done = bf16[8,32,4,256]{3,2,0,1:T(4,128)(2,1)S(1)} async-done(((bf16[8,32,4,256]{3,2,0,1:T(4,128)(2,1)}), bf16[8,32,4,256]{3,2,0,1:T(4,128)(2,1)S(1)}, u32[]{:S(2)}, u32[]{:S(2)}) %all-to-all-start) | async-done | bytes 524320 | tf_op jit(solution)/shard_map/all_to_all | solution.py:92
  145.1 113.5 %while.22 = (s32[]{:T(128)}, f32[16]{0:T(128)S(1)}, s32[16,1024]{1,0:T(8,128)}, bf16[128,256]{1,0:T(8,128)(2,1)S(1)}, f32[1024,256]{1,0:T(8,128)S(1)}, /*index=5...) while((s32[]{:T(128)}, f32[16]{0:T(128)S(1)}, ...), condition=%wide.region_2.4_spmd.clone, body=%wide.region_0.3_spmd.clone.sunk | while | flops 207750144 | bytes 3366021 | solution.py:108
  160.1 2.5 convolution_add_fusion.6
  174.3 2.5 convolution_add_fusion.6
  195.6 2.5 convolution_add_fusion.6
  216.8 2.5 convolution_add_fusion.6
  245.2 2.5 convolution_add_fusion.6
  258.7 70.7 %psum.7 = f32[16]{0:T(128)S(1)} all-reduce(f32[16]{0:T(128)S(1)} %get-tuple-element.114), channel_id=1, replica_groups=mesh['cfg'=8,'node'=32] {'node'}, use_global_device_ids=true, to_apply=%region_3.5 | all-reduce | flops 16 | bytes 128 | tf_op jit(solution)/shard_map/psum | solution.py:109
  329.5 12.4 %all-reduce = f32[128]{0:T(128)S(1)} all-reduce(f32[128]{0:T(128)S(1)} %multiply_dynamic-update-slice_fusion), channel_id=1, replica_groups=mesh['cfg'=8,'node'=32] {'cfg'}, use_global_device_ids=true, to_apply=%add | all-reduce | flops 128 | bytes 1024
  341.9 3.3 gather_fusion.5
  345.2 3.3 gather_fusion.6
  349.1 72.5 %while.23 = (s32[]{:T(128)}, f32[1024,256]{1,0:T(8,128)S(1)}, f32[16]{0:T(128)S(1)}, f32[256]{0:T(256)S(1)}, s32[16,1024]{1,0:T(8,128)}, /*index=5*/bf16[128,256...) while((s32[]{:T(128)}, f32[1024,256]{1,0:T(8,128)S(1)}, ...), condition=%wide.region_6.9_spmd.clone, body=%wide.region_5.8_spmd.clone.sunk | while | flops 342753536 | bytes 5457063 | solution.py:128
  422.4 28.7 %reduce-scatter.2.cloned.1.call-done = bf16[128,256]{1,0:T(8,128)(2,1)} async-done(((bf16[1024,256]{1,0:T(8,128)(2,1)}), bf16[128,256]{1,0:T(8,128)(2,1)}) %reduce-scatter.2.cloned.1.call-update) | async-done | bytes 65552 | tf_op jit(solution)/shard_map/reduce_scatter | solution.py:129
  452.8 10.2 %all-to-all-start.1 = ((bf16[32,4,256]{2,1,0:T(4,128)(2,1)}), bf16[32,4,256]{2,1,0:T(4,128)(2,1)S(1)}, u32[]{:S(2)}, u32[]{:S(2)}) async-start(bf16[32,4,256]{2,1,0:T(4,128)(2,1)} %convert_element_type.55), calls=%async_computation.2 | async-start | bytes 131072 | tf_op jit(solution)/shard_map/all_to_all | solution.py:135
  464.3 7.4 %all-to-all-done.1 = bf16[32,4,256]{2,1,0:T(4,128)(2,1)S(1)} async-done(((bf16[32,4,256]{2,1,0:T(4,128)(2,1)}), bf16[32,4,256]{2,1,0:T(4,128)(2,1)S(1)}, u32[]{:S(2)}, u32[]{:S(2)}) %all-to-all-start.1) | async-done | bytes 65568 | tf_op jit(solution)/shard_map/all_to_all | solution.py:135
  (222 shorter events, 176.9 us)
Async XLA Ops:
  7.2 9.4 %copy-start = (bf16[256,256]{1,0:T(8,128)(2,1)S(1)}, bf16[256,256]{1,0:T(8,128)(2,1)}, u32[]{:S(2)}) copy-start(bf16[256,256]{1,0:T(8,128)(2,1)} %param.24) | copy-start | bytes 393220
  8.3 12.8 %collective-permute-start = (bf16[512,256]{1,0:T(8,128)(2,1)S(1)}, bf16[512,256]{1,0:T(8,128)(2,1)S(1)}, u32[]{:S(2)}, u32[]{:S(2)}) collective-permute-start(bf16[512,256]{1,0:T(8,128)(2,1)S(1)} %get-tuple-element.212), channel_id=1, source_target_pairs={{0,1},{1,2},{2,3},{3,4},{4,5},{5,6},{6,7},{7,8},{8,9},{9,10},{10,1... | collective-permute-start | bytes 786440 | tf_op jit(solution)/shard_map/ppermute | solution.py:17
  11.7 9.7 %collective-permute-start.1 = (bf16[512,256]{1,0:T(8,128)(2,1)S(1)}, bf16[512,256]{1,0:T(8,128)(2,1)S(1)}, u32[]{:S(2)}, u32[]{:S(2)}) collective-permute-start(bf16[512,256]{1,0:T(8,128)(2,1)S(1)} %get-tuple-element.211), channel_id=1, source_target_pairs={{1,0},{2,1},{3,2},{4,3},{5,4},{6,5},{7,6},{8,7},{9,8},{10,9},{11,1... | collective-permute-start | bytes 786440 | tf_op jit(solution)/shard_map/ppermute | solution.py:18
  16.6 4.5 copy-start.1
  72.2 16.9 %copy-start.8 = (bf16[256,256]{1,0:T(8,128)(2,1)S(1)}, bf16[256,256]{1,0:T(8,128)(2,1)}, u32[]{:S(2)}) copy-start(bf16[256,256]{1,0:T(8,128)(2,1)} %param.25) | copy-start | bytes 393220
  72.2 16.9 %copy-start.9 = (f32[256]{0:T(256)S(1)}, f32[256]{0:T(256)}, u32[]{:S(2)}) copy-start(f32[256]{0:T(256)} %param.26) | copy-start | bytes 3076
  97.2 1.3 copy-start.4
  97.2 30.0 %copy-start.11 = (u32[256]{0:T(256)S(1)}, u32[256]{0:T(256)}, u32[]{:S(2)}) copy-start(u32[256]{0:T(256)} %constant.97) | copy-start | bytes 3076
  98.5 30.0 %copy-start.7 = (s32[512,2]{0,1:T(2,128)S(1)}, s32[512,2]{0,1:T(2,128)}, u32[]{:S(2)}) copy-start(s32[512,2]{0,1:T(2,128)} %param.35) | copy-start | bytes 12292
  112.4 32.4 %copy-start.3 = (bf16[256,256]{1,0:T(8,128)(2,1)S(1)}, bf16[256,256]{1,0:T(8,128)(2,1)}, u32[]{:S(2)}) copy-start(bf16[256,256]{1,0:T(8,128)(2,1)} %param.29) | copy-start | bytes 393220
  113.4 31.0 %all-to-all-start = ((bf16[8,32,4,256]{3,2,0,1:T(4,128)(2,1)}), bf16[8,32,4,256]{3,2,0,1:T(4,128)(2,1)S(1)}, u32[]{:S(2)}, u32[]{:S(2)}) async-start(bf16[8,32,4,256]{3,2,0,1:T(4,128)(2,1)} %copy.18), calls=%async_computation | async-start | bytes 1048576 | tf_op jit(solution)/shard_map/all_to_all | solution.py:92
  127.1 18.0 %copy-start.2 = (bf16[128,256]{1,0:T(8,128)(2,1)S(1)}, bf16[128,256]{1,0:T(8,128)(2,1)}, u32[]{:S(2)}) copy-start(bf16[128,256]{1,0:T(8,128)(2,1)} %param.30) | copy-start | bytes 196612
  127.1 18.0 %copy-start.5 = (f32[256]{0:T(256)S(1)}, f32[256]{0:T(256)}, u32[]{:S(2)}) copy-start(f32[256]{0:T(256)} %param.31) | copy-start | bytes 3076
  127.1 18.0 %copy-start.6 = (f32[256]{0:T(256)S(1)}, f32[256]{0:T(256)}, u32[]{:S(2)}) copy-start(f32[256]{0:T(256)} %param.34) | copy-start | bytes 3076
  127.1 18.0 %copy-start.10 = (f32[256]{0:T(256)S(1)}, f32[256]{0:T(256)}, u32[]{:S(2)}) copy-start(f32[256]{0:T(256)} %param.33) | copy-start | bytes 3076
  127.2 324.0 %reduce-scatter.2.cloned.1.call-start = ((), (), s32[]{:S(2)}) async-start(), calls=%async_computation.3 | async-start | bytes 589824 | tf_op jit(solution)/shard_map/reduce_scatter | solution.py:129
  452.8 18.9 %all-to-all-start.1 = ((bf16[32,4,256]{2,1,0:T(4,128)(2,1)}), bf16[32,4,256]{2,1,0:T(4,128)(2,1)S(1)}, u32[]{:S(2)}, u32[]{:S(2)}) async-start(bf16[32,4,256]{2,1,0:T(4,128)(2,1)} %convert_element_type.55), calls=%async_computation.2 | async-start | bytes 131072 | tf_op jit(solution)/shard_map/all_to_all | solution.py:135
Sparse Core Ops, SparseCore 0:
  422.5 28.5 reduce-scatter.1
where the time goes:
time: 485 us; the launch traced here: 480 us
  matrix products  132 us (27%)
  local copies, waits for them, and re-layouts  127 us (26%)
  blocking collectives  96.7 us (20%)
  waiting for transfers between devices  52.2 us (11%)
  starting transfers between devices  29.8 us (6%)
  between operations  16.9 us (3%)
  other arithmetic  14 us (3%)
  loops' own time  11.2 us (2%)
    psum x1, blocking collectives, shards(): local_score = lax.psum(partial_sums, 'node') * norm_scale  70.7 us
    gather x4, local copies, waits for them, and re-layouts, shards(): jnp.take(padded, neighbors[:, neighbor], axis=0).astype(jnp.float32)  67.7 us
    dot_general x16, matrix products, hidden_rows(): jnp.dot(inner_act, mid_weight, preferred_element_type=jnp.float32)  40 us
    dot_general x16, matrix products, config_total(): jnp.dot(jax.nn.silu(outer_pre), score_weight, precision=lax.Precision.HIG...  38.7 us
    dot_general x16, matrix products, config_step(): lax.dot_general(outer_grad, mid_weight, (((1,), (1,)), ((), ())), preferr...  33.9 us
    reduce_scatter x1, waiting for transfers between devices, shards(): lax.psum_scatter(group_part.astype(jnp.bfloat16), 'cfg', scatter_dimensio...  28.7 us
    dynamic_slice x32, local copies, waits for them, and re-layouts, shards(): partial_sums = lax.map(config_total, layout_ids)  24.5 us
    all_to_all x1, waiting for transfers between devices, shards(): lax.all_to_all(grouped.reshape(group_count, node_count, per_peer, feat_wi...  15.9 us
  transfers between devices with their start and end apart: 5, of which 4 were waited for; matrix products, arithmetic and copies ran while one was open for 2% of the time, Pallas kernels for 0%

commit v1 on v0

--- a/solution.py
+++ b/solution.py
@@ -88,7 +88,9 @@
         outer_pre = jnp.dot(inner_act, mid_weight, preferred_element_type=jnp.float32) + mid_bias
         return (inner_pre, outer_pre)
 
-    grouped = lax.all_gather(conf_src, "cfg", axis=0, tiled=True)
+    grouped = jnp.concatenate(
+        lax.all_to_all(jnp.stack([conf_src] * lax.axis_size("cfg")), "cfg", 0, 0), axis=0
+    )
     spread = lax.all_to_all(
         grouped.reshape(group_count, node_count, per_peer, feat_width),
         "node",

time: 485 us -> 485 us (level)
    all_to_all x0 -> x1, blocking collectives: none -> 14.7 us  [shards(): lax.all_to_all(jnp.stack([conf_src] * lax.axis_size('cfg')), 'cfg', 0, 0)]
    all_gather x1 -> x0, blocking collectives: 13.6 us -> none  [shards(): grouped = lax.all_gather(conf_src, 'cfg', axis=0, tiled=True)]
where the time goes in v1:
time: 485 us; the launch traced here: 480 us
  matrix products  132 us (27%)
  local copies, waits for them, and re-layouts  127 us (26%)
  blocking collectives  97.9 us (20%)
  waiting for transfers between devices  51.3 us (11%)
  starting transfers between devices  29.7 us (6%)
  between operations  16.9 us (3%)
  other arithmetic  14 us (3%)
  loops' own time  11.2 us (2%)
    psum x1, blocking collectives, shards(): local_score = lax.psum(partial_sums, 'node') * norm_scale  70.8 us
    gather x4, local copies, waits for them, and re-layouts, shards(): jnp.take(padded, neighbors[:, neighbor], axis=0).astype(jnp.float32)  67.7 us
    dot_general x16, matrix products, hidden_rows(): jnp.dot(inner_act, mid_weight, preferred_element_type=jnp.float32)  40 us
    dot_general x16, matrix products, config_total(): jnp.dot(jax.nn.silu(outer_pre), score_weight, precision=lax.Precision.HIG...  38.7 us
    dot_general x16, matrix products, config_step(): lax.dot_general(outer_grad, mid_weight, (((1,), (1,)), ((), ())), preferr...  33.9 us
    reduce_scatter x1, waiting for transfers between devices, shards(): lax.psum_scatter(group_part.astype(jnp.bfloat16), 'cfg', scatter_dimensio...  28.7 us
    dynamic_slice x32, local copies, waits for them, and re-layouts, shards(): partial_sums = lax.map(config_total, layout_ids)  24.5 us
    all_to_all x1, waiting for transfers between devices, shards(): lax.all_to_all(grouped.reshape(group_count, node_count, per_peer, feat_wi...  15 us
  transfers between devices with their start and end apart: 5, of which 4 were waited for; matrix products, arithmetic and copies ran while one was open for 2% of the time, Pallas kernels for 0%

profile of v1, /device:TPU:2, one launch (start us, length us, event | category | flops | bytes accessed | tf_op | source)
XLA Modules:
  0.0 480.3 jit_solution(6353628002819623985)
XLA Ops:
  8.3 3.4 collective-permute-start
  16.6 4.4 fusion.62
  21.4 17.0 %gather_fusion.4 = bf16[4096,256]{1,0:T(8,128)(2,1)} fusion(bf16[5120,256]{1,0:T(8,128)(2,1)S(1)} %constant_dynamic-update-slice_fusion, s32[4096]{0:T(1024)S(1)} %fusion.55), kind=kCustom, calls=%fused_computation.4.clone | custom fusion | bytes 4210688 | tf_op jit(solution)/shard_map/jit(_take)/gather | solution.py:65
  38.4 16.9 %gather_fusion.1 = bf16[4096,256]{1,0:T(8,128)(2,1)} fusion(bf16[5120,256]{1,0:T(8,128)(2,1)S(1)} %constant_dynamic-update-slice_fusion, s32[4096]{0:T(1024)S(1)} %fusion.52), kind=kCustom, calls=%fused_computation.clone | custom fusion | bytes 4210688 | tf_op jit(solution)/shard_map/jit(_take)/gather | solution.py:65
  55.3 16.9 %gather_fusion.2 = bf16[4096,256]{1,0:T(8,128)(2,1)} fusion(bf16[5120,256]{1,0:T(8,128)(2,1)S(1)} %constant_dynamic-update-slice_fusion, s32[4096]{0:T(1024)S(1)} %fusion.53), kind=kCustom, calls=%fused_computation.2.clone | custom fusion | bytes 4210688 | tf_op jit(solution)/shard_map/jit(_take)/gather | solution.py:65
  72.2 16.9 %gather_fusion.3 = bf16[4096,256]{1,0:T(8,128)(2,1)} fusion(bf16[5120,256]{1,0:T(8,128)(2,1)S(1)} %constant_dynamic-update-slice_fusion, s32[4096]{0:T(1024)S(1)} %fusion.54), kind=kCustom, calls=%fused_computation.3.clone | custom fusion | bytes 4210688 | tf_op jit(solution)/shard_map/jit(_take)/gather | solution.py:65
  89.1 8.0 %multiply_convert_fusion.5 = bf16[4096,256]{1,0:T(8,128)(2,1)S(1)} fusion(f32[4096,256]{1,0:T(8,128)} %fusion.62, bf16[256,256]{1,0:T(8,128)(2,1)S(1)} %copy-done.8, bf16[4096,256]{1,0:T(8,128)(2,1)} %gather_fusion.4, bf16[4096,256]{1,0:T(8,128)(2,1)} %gather_fusion.3, bf16[4096,256]{1,0:T(8,128)(2,1)} %gather_fusion.2, ...), kind=kOutput, calls=%fused_computation.48 | convolution fusion | flops 557842432 | bytes 14828544 | tf_op jit(solution)/shard_map/dot_general | solution.py:69
  98.2 14.7 %all_to_all.15 = bf16[8,128,256]{2,1,0:T(8,128)(2,1)S(1)} all-to-all(bf16[8,128,256]{2,1,0:T(8,128)(2,1)S(1)} %stack.2), channel_id=1, replica_groups=mesh['cfg'=8,'node'=32] {'cfg'}, dimensions={0} | all-to-all | bytes 1048576 | tf_op jit(solution)/shard_map/all_to_all | solution.py:92
  114.2 13.7 %all-to-all-start.1 = ((bf16[8,32,4,256]{3,2,0,1:T(4,128)(2,1)}), bf16[8,32,4,256]{3,2,0,1:T(4,128)(2,1)S(1)}, u32[]{:S(2)}, u32[]{:S(2)}) async-start(bf16[8,32,4,256]{3,2,0,1:T(4,128)(2,1)} %copy.20), calls=%async_computation.1 | async-start | bytes 1048576 | tf_op jit(solution)/shard_map/all_to_all | solution.py:94
  129.3 15.0 %all-to-all-done.1 = bf16[8,32,4,256]{3,2,0,1:T(4,128)(2,1)S(1)} async-done(((bf16[8,32,4,256]{3,2,0,1:T(4,128)(2,1)}), bf16[8,32,4,256]{3,2,0,1:T(4,128)(2,1)S(1)}, u32[]{:S(2)}, u32[]{:S(2)}) %all-to-all-start.1) | async-done | bytes 524320 | tf_op jit(solution)/shard_map/all_to_all | solution.py:94
  145.0 113.5 %while.22 = (s32[]{:T(128)}, f32[16]{0:T(128)S(1)}, s32[16,1024]{1,0:T(8,128)}, bf16[128,256]{1,0:T(8,128)(2,1)S(1)}, f32[1024,256]{1,0:T(8,128)S(1)}, /*index=5...) while((s32[]{:T(128)}, f32[16]{0:T(128)S(1)}, ...), condition=%wide.region_2.4_spmd.clone, body=%wide.region_0.3_spmd.clone.sunk | while | flops 207750144 | bytes 3366021 | solution.py:110
  152.9 2.5 convolution_add_fusion.6
  167.1 2.5 convolution_add_fusion.6
  188.4 2.5 convolution_add_fusion.6
  202.6 2.5 convolution_add_fusion.6
  216.8 2.5 convolution_add_fusion.6
  258.6 70.8 %psum.7 = f32[16]{0:T(128)S(1)} all-reduce(f32[16]{0:T(128)S(1)} %get-tuple-element.114), channel_id=1, replica_groups=mesh['cfg'=8,'node'=32] {'node'}, use_global_device_ids=true, to_apply=%region_3.5 | all-reduce | flops 16 | bytes 128 | tf_op jit(solution)/shard_map/psum | solution.py:111
  329.5 12.4 %all-reduce = f32[128]{0:T(128)S(1)} all-reduce(f32[128]{0:T(128)S(1)} %multiply_dynamic-update-slice_fusion), channel_id=1, replica_groups=mesh['cfg'=8,'node'=32] {'cfg'}, use_global_device_ids=true, to_apply=%add | all-reduce | flops 128 | bytes 1024
  341.9 3.3 gather_fusion.5
  345.2 3.3 gather_fusion.6
  349.1 72.5 %while.23 = (s32[]{:T(128)}, f32[1024,256]{1,0:T(8,128)S(1)}, f32[16]{0:T(128)S(1)}, f32[256]{0:T(256)S(1)}, s32[16,1024]{1,0:T(8,128)}, /*index=5*/bf16[128,256...) while((s32[]{:T(128)}, f32[1024,256]{1,0:T(8,128)S(1)}, ...), condition=%wide.region_6.9_spmd.clone, body=%wide.region_5.8_spmd.clone.sunk | while | flops 342753536 | bytes 5457063 | solution.py:130
  422.4 28.7 %reduce-scatter.2.cloned.1.call-done = bf16[128,256]{1,0:T(8,128)(2,1)} async-done(((bf16[1024,256]{1,0:T(8,128)(2,1)}), bf16[128,256]{1,0:T(8,128)(2,1)}) %reduce-scatter.2.cloned.1.call-update) | async-done | bytes 65552 | tf_op jit(solution)/shard_map/reduce_scatter | solution.py:131
  452.8 10.1 %all-to-all-start.2 = ((bf16[32,4,256]{2,1,0:T(4,128)(2,1)}), bf16[32,4,256]{2,1,0:T(4,128)(2,1)S(1)}, u32[]{:S(2)}, u32[]{:S(2)}) async-start(bf16[32,4,256]{2,1,0:T(4,128)(2,1)} %convert_element_type.55), calls=%async_computation.3 | async-start | bytes 131072 | tf_op jit(solution)/shard_map/all_to_all | solution.py:137
  464.2 7.4 %all-to-all-done.2 = bf16[32,4,256]{2,1,0:T(4,128)(2,1)S(1)} async-done(((bf16[32,4,256]{2,1,0:T(4,128)(2,1)}), bf16[32,4,256]{2,1,0:T(4,128)(2,1)S(1)}, u32[]{:S(2)}, u32[]{:S(2)}) %all-to-all-start.2) | async-done | bytes 65568 | tf_op jit(solution)/shard_map/all_to_all | solution.py:137
  (223 shorter events, 176.7 us)
Async XLA Ops:
  7.2 9.4 %copy-start = (bf16[256,256]{1,0:T(8,128)(2,1)S(1)}, bf16[256,256]{1,0:T(8,128)(2,1)}, u32[]{:S(2)}) copy-start(bf16[256,256]{1,0:T(8,128)(2,1)} %param.24) | copy-start | bytes 393220
  8.3 12.8 %collective-permute-start = (bf16[512,256]{1,0:T(8,128)(2,1)S(1)}, bf16[512,256]{1,0:T(8,128)(2,1)S(1)}, u32[]{:S(2)}, u32[]{:S(2)}) collective-permute-start(bf16[512,256]{1,0:T(8,128)(2,1)S(1)} %get-tuple-element.212), channel_id=1, source_target_pairs={{0,1},{1,2},{2,3},{3,4},{4,5},{5,6},{6,7},{7,8},{8,9},{9,10},{10,1... | collective-permute-start | bytes 786440 | tf_op jit(solution)/shard_map/ppermute | solution.py:17
  11.7 9.7 %collective-permute-start.1 = (bf16[512,256]{1,0:T(8,128)(2,1)S(1)}, bf16[512,256]{1,0:T(8,128)(2,1)S(1)}, u32[]{:S(2)}, u32[]{:S(2)}) collective-permute-start(bf16[512,256]{1,0:T(8,128)(2,1)S(1)} %get-tuple-element.211), channel_id=1, source_target_pairs={{1,0},{2,1},{3,2},{4,3},{5,4},{6,5},{7,6},{8,7},{9,8},{10,9},{11,1... | collective-permute-start | bytes 786440 | tf_op jit(solution)/shard_map/ppermute | solution.py:18
  16.6 4.5 copy-start.1
  72.2 16.9 %copy-start.8 = (bf16[256,256]{1,0:T(8,128)(2,1)S(1)}, bf16[256,256]{1,0:T(8,128)(2,1)}, u32[]{:S(2)}) copy-start(bf16[256,256]{1,0:T(8,128)(2,1)} %param.25) | copy-start | bytes 393220
  72.2 16.9 %copy-start.9 = (f32[256]{0:T(256)S(1)}, f32[256]{0:T(256)}, u32[]{:S(2)}) copy-start(f32[256]{0:T(256)} %param.26) | copy-start | bytes 3076
  97.2 17.0 %copy-start.4 = (bf16[4096,256]{1,0:T(8,128)(2,1)}, bf16[4096,256]{1,0:T(8,128)(2,1)S(1)}, u32[]{:S(2)}) copy-start(bf16[4096,256]{1,0:T(8,128)(2,1)S(1)} %multiply_convert_fusion.5) | copy-start | bytes 6291460
  98.2 29.8 %copy-start.11 = (u32[256]{0:T(256)S(1)}, u32[256]{0:T(256)}, u32[]{:S(2)}) copy-start(u32[256]{0:T(256)} %constant.97) | copy-start | bytes 3076
  98.2 31.1 %copy-start.7 = (s32[512,2]{0,1:T(2,128)S(1)}, s32[512,2]{0,1:T(2,128)}, u32[]{:S(2)}) copy-start(s32[512,2]{0,1:T(2,128)} %param.35) | copy-start | bytes 12292
  113.2 31.5 %copy-start.3 = (bf16[256,256]{1,0:T(8,128)(2,1)S(1)}, bf16[256,256]{1,0:T(8,128)(2,1)}, u32[]{:S(2)}) copy-start(bf16[256,256]{1,0:T(8,128)(2,1)} %param.29) | copy-start | bytes 393220
  114.2 30.1 %all-to-all-start.1 = ((bf16[8,32,4,256]{3,2,0,1:T(4,128)(2,1)}), bf16[8,32,4,256]{3,2,0,1:T(4,128)(2,1)S(1)}, u32[]{:S(2)}, u32[]{:S(2)}) async-start(bf16[8,32,4,256]{3,2,0,1:T(4,128)(2,1)} %copy.20), calls=%async_computation.1 | async-start | bytes 1048576 | tf_op jit(solution)/shard_map/all_to_all | solution.py:94
  127.9 17.1 %copy-start.2 = (bf16[128,256]{1,0:T(8,128)(2,1)S(1)}, bf16[128,256]{1,0:T(8,128)(2,1)}, u32[]{:S(2)}) copy-start(bf16[128,256]{1,0:T(8,128)(2,1)} %param.30) | copy-start | bytes 196612
  127.9 17.1 %copy-start.5 = (f32[256]{0:T(256)S(1)}, f32[256]{0:T(256)}, u32[]{:S(2)}) copy-start(f32[256]{0:T(256)} %param.31) | copy-start | bytes 3076
  127.9 17.1 %copy-start.6 = (f32[256]{0:T(256)S(1)}, f32[256]{0:T(256)}, u32[]{:S(2)}) copy-start(f32[256]{0:T(256)} %param.34) | copy-start | bytes 3076
  127.9 17.1 %copy-start.10 = (f32[256]{0:T(256)S(1)}, f32[256]{0:T(256)}, u32[]{:S(2)}) copy-start(f32[256]{0:T(256)} %param.33) | copy-start | bytes 3076
  127.9 323.2 %reduce-scatter.2.cloned.1.call-start = ((), (), s32[]{:S(2)}) async-start(), calls=%async_computation.4 | async-start | bytes 589824 | tf_op jit(solution)/shard_map/reduce_scatter | solution.py:131
  452.8 18.8 %all-to-all-start.2 = ((bf16[32,4,256]{2,1,0:T(4,128)(2,1)}), bf16[32,4,256]{2,1,0:T(4,128)(2,1)S(1)}, u32[]{:S(2)}, u32[]{:S(2)}) async-start(bf16[32,4,256]{2,1,0:T(4,128)(2,1)} %convert_element_type.55), calls=%async_computation.3 | async-start | bytes 131072 | tf_op jit(solution)/shard_map/all_to_all | solution.py:137
Sparse Core Ops, SparseCore 0:
  422.6 28.5 reduce-scatter.1
